TPU v7x, 512 devices: a whole 4x8x8 slice. The times are simulated.
512 devices in a mesh: ctx: 64 (over y_hi, z, core), tp: 8 (over x, y_lo).
Axes of the slice: x: 4, y: 8 (y_hi: 4, y_lo: 2; y = y_hi * 2 + y_lo), z: 8, core: 2. Of those that a mesh axis runs over, the one named last changes fastest.
Arguments:
- q_new: bfloat16 [1024, 8192], P(('ctx', 'tp')), may hold values from -128 to 128
- kv_new: bfloat16 [2, 1024, 1024], P(None, 'ctx', 'tp'), may hold values from -4 to 4
- kv_cache: bfloat16 [2, 31744, 1024], P(None, 'ctx', 'tp'), may hold values from -4 to 4
- cache_lens: int32 [64], replicated, may hold values from 1 to 496, 15872 in all
- segment_ids: int32 [1024], replicated, may hold values from 0 to 63, never falling along the last dimension, each value on 1 to 32 neighbouring positions
Outputs:
- attn_out: bfloat16 [1024, 8192], P(('ctx', 'tp'))
- attn_lse: float32 [1024, 64], P('ctx', 'tp')
Inputs may be any that keep to these rules, and one draw needn't show every extreme that they name: The filled slots of shard c are its first cache_lens[c] slots; the lengths sum to 15872 and some shard is full. `segment_ids`: never falls along the turn; a segment holds at most 32 tokens, and some segment exactly 32.
All inputs are finite; a program needn't handle non-finite values.
Results may differ from a plain program's by a relative error of at most 0.0015.
Values may be sent and summed in bfloat16 or wider, within the bound.
No kernel may reach another device: no remote copies, remote signals or barrier semaphores. Data moves between devices by JAX's collectives and lax.ppermute only.
A program may use at most 64 MiB of HBM per device.

v0:
```python
import jax
import jax.numpy as jnp
from jax import lax
from jax.sharding import PartitionSpec as P


def shard_partial(queries, query_seg, keys_all, values_all, filled, key_seg, head_dim):
    rows = queries.shape[0]
    heads = queries.shape[1] // head_dim
    total = keys_all.shape[0]
    cache_count = total - key_seg.shape[0]
    flat = queries.reshape(rows * heads, head_dim)
    scores = lax.dot_general(
        flat, keys_all, (((1,), (1,)), ((), ())), preferred_element_type=jnp.float32
    ) * head_dim ** (-0.5)
    scores = scores.reshape(rows, heads, total)
    slot_rank = jnp.where(jnp.arange(cache_count) < filled, -1, 2**30).astype(jnp.int32)
    key_rank = jnp.concatenate([slot_rank, key_seg])
    visible = key_rank[None, None, :] <= query_seg[:, None, None]
    masked = jnp.where(visible, scores, -jnp.inf)
    peak = jnp.max(masked, axis=2)
    expo = jnp.exp(masked - peak[:, :, None])
    denom = jnp.sum(expo, axis=2)
    weights = expo.astype(jnp.bfloat16).reshape(rows * heads, total)
    mixed = jnp.dot(weights, values_all, preferred_element_type=jnp.float32)
    mixed = mixed.reshape(rows, heads, head_dim) / denom[:, :, None]
    return (mixed.reshape(rows, heads * head_dim), peak + jnp.log(denom))


def shards(q_new, kv_new, kv_cache, cache_lens, segment_ids):
    head_dim = kv_cache.shape[2]
    block = kv_new.shape[1]
    here = lax.axis_index("ctx")
    count = lax.axis_size("ctx")
    queries = lax.all_to_all(q_new, "tp", split_axis=1, concat_axis=0, tiled=True)
    heads = queries.shape[1] // head_dim
    keys_all = jnp.concatenate([kv_cache[0], kv_new[0]])
    values_all = jnp.concatenate([kv_cache[1], kv_new[1]])
    filled = cache_lens[here]
    key_seg = lax.dynamic_slice_in_dim(segment_ids, here * block, block, 0)
    total_rows = block * count
    init = (
        jnp.zeros((total_rows, heads * head_dim), jnp.float32),
        jnp.zeros((total_rows, heads), jnp.float32),
    )
    piece = lax.all_gather(queries, "ctx", axis=0, tiled=True)
    rows = piece.shape[0]
    width = 64

    def one_block(index, inner):
        outs, lses = inner
        offset = index * width
        part = lax.dynamic_slice_in_dim(piece, index * width, width, 0)
        part_seg = lax.dynamic_slice_in_dim(segment_ids, offset, width, 0)
        mixed, lse = shard_partial(part, part_seg, keys_all, values_all, filled, key_seg, head_dim)
        outs = lax.dynamic_update_slice_in_dim(outs, mixed, offset, 0)
        lses = lax.dynamic_update_slice_in_dim(lses, lse, offset, 0)
        return (outs, lses)

    partial_out, partial_lse = lax.fori_loop(0, rows // width, one_block, init)
    got_out, got_lse = (
        lax.all_to_all(
            partial_out.reshape(count, block, heads * head_dim),
            "ctx",
            split_axis=0,
            concat_axis=0,
            tiled=True,
        ),
        lax.all_to_all(
            partial_lse.reshape(count, block, heads), "ctx", split_axis=0, concat_axis=0, tiled=True
        ),
    )
    peak = jnp.max(got_lse, axis=0)
    scale = jnp.exp(got_lse - peak[None])
    denom = jnp.sum(scale, axis=0)
    numer = jnp.sum(got_out.reshape(count, block, heads, head_dim) * scale[:, :, :, None], axis=0)
    final = (numer / denom[:, :, None]).reshape(block, heads * head_dim)
    lse_out = peak + jnp.log(denom)
    attn_out = lax.all_to_all(
        final.astype(jnp.bfloat16), "tp", split_axis=0, concat_axis=1, tiled=True
    )
    return (attn_out, lse_out)


def solution(mesh):
    return jax.shard_map(
        shards,
        mesh=mesh,
        in_specs=(P(("ctx", "tp"), None), P(None, "ctx", "tp"), P(None, "ctx", "tp"), P(), P()),
        out_specs=(P(("ctx", "tp"), None), P("ctx", "tp")),
        check_vma=False,
    )
```

profile of v0, /device:TPU:272, one launch (start us, length us, event | category | flops | bytes accessed | tf_op | source)
XLA Modules:
  0.0 346.2 jit_solution(2459077010839411977)
XLA Ops:
  7.2 11.6 %all_to_all.45 = bf16[2,8,1024]{2,0,1:T(2,128)(2,1)S(1)} all-to-all(bf16[2,8,1024]{2,0,1:T(2,128)(2,1)} %bitcast.53), channel_id=1, replica_groups=mesh['ctx'=64,'tp'=8] {'tp'}, dimensions={1} | all-to-all | bytes 65536 | tf_op jit(solution)/shard_map/all_to_all | solution.py:35
  19.5 1.2 dynamic_slice.20
  22.2 1.0 slice_bitcast_fusion
  23.2 76.2 %all-gather.2.cloned.1.call-done = bf16[1024,1024]{1,0:T(8,128)(2,1)} async-done(((bf16[16,1024]{1,0:T(8,128)(2,1)}), bf16[1024,1024]{1,0:T(8,128)(2,1)}) %all-gather.2.cloned.1.call-update) | async-done | bytes 2097168 | tf_op jit(solution)/shard_map/all_gather | solution.py:46
  99.4 2.5 broadcast_in_dim.61
  102.0 74.2 %while.15 = (s32[]{:T(128)}, f32[1024,1024]{1,0:T(8,128)}, f32[1024,8]{1,0:T(8,128)S(1)}, s32[]{:T(128)}, s32[16]{0:T(128)S(1)}, /*index=5*/s32[1024]{0:T(1024)}...) while((s32[]{:T(128)}, f32[1024,1024]{1,0:T(8,128)}, ...), condition=%wide.region_3.4_spmd, body=%wide.region_0.3_spmd.sunk | while | flops 136152032 | bytes 5041031 | solution.py:60
  102.0 0.9 constant_dynamic-slice_fusion.2
  106.6 0.9 constant_dynamic-slice_fusion.2
  111.2 0.9 constant_dynamic-slice_fusion.2
  115.0 0.8 bitcast_dynamic-update-slice_fusion.2
  115.9 0.9 constant_dynamic-slice_fusion.2
  119.6 0.8 bitcast_dynamic-update-slice_fusion.2
  120.5 0.9 constant_dynamic-slice_fusion.2
  125.2 0.9 constant_dynamic-slice_fusion.2
  129.8 0.9 constant_dynamic-slice_fusion.2
  134.5 0.9 constant_dynamic-slice_fusion.2
  139.1 0.9 constant_dynamic-slice_fusion.2
  143.8 0.9 constant_dynamic-slice_fusion.2
  148.4 0.9 constant_dynamic-slice_fusion.2
  153.0 0.9 constant_dynamic-slice_fusion.2
  157.7 0.9 constant_dynamic-slice_fusion.2
  162.3 0.9 constant_dynamic-slice_fusion.2
  166.9 0.9 constant_dynamic-slice_fusion.2
  171.5 0.9 constant_dynamic-slice_fusion.2
  176.5 16.2 %all_to_all.46 = f32[64,1,128]{2,1,0:T(1,128)S(1)} all-to-all(f32[64,1,128]{2,1,0:T(1,128)S(1)} %reshape.108), channel_id=1, replica_groups=mesh['ctx'=64,'tp'=8] {'ctx'}, dimensions={0} | all-to-all | bytes 65536 | tf_op jit(solution)/shard_map/all_to_all | solution.py:69
  192.7 12.0 %all-to-all-start.1 = ((f32[64,16,1024]{2,1,0:T(8,128)}), f32[64,16,1024]{2,1,0:T(8,128)}, u32[]{:S(2)}, u32[]{:S(2)}) async-start(f32[64,16,1024]{2,1,0:T(8,128)} %bitcast.46), calls=%async_computation.1 | async-start | bytes 8388608 | tf_op jit(solution)/shard_map/all_to_all | solution.py:62
  206.9 2.6 mul.30
  209.4 4.9 %mul.31 = f32[64,16,1024]{2,1,0:T(8,128)} reshape(f32[64,16,8,128]{3,2,1,0:T(8,128)} %mul.30) | data formatting | bytes 8388608 | tf_op jit(solution)/shard_map/mul | solution.py:76
  214.5 109.1 %all-to-all-done.1 = f32[64,16,1024]{2,1,0:T(8,128)} async-done(((f32[64,16,1024]{2,1,0:T(8,128)}), f32[64,16,1024]{2,1,0:T(8,128)}, u32[]{:S(2)}, u32[]{:S(2)}) %all-to-all-start.1) | async-done | bytes 4194336 | tf_op jit(solution)/shard_map/all_to_all | solution.py:62
  323.6 4.0 %multiply_reduce_fusion = f32[16,1024]{1,0:T(8,128)S(1)} fusion(f32[64,16,1024]{2,1,0:T(8,128)} %all-to-all-done.1, f32[64,16,1024]{2,1,0:T(8,128)} %mul.31), kind=kLoop, calls=%fused_computation.16 | loop fusion | flops 2080768 | bytes 8454144 | tf_op jit(solution)/shard_map/reduce_sum | solution.py:76
  328.2 4.3 %all-to-all-start.3 = ((bf16[8,2,1024]{2,1,0:T(2,128)(2,1)}), bf16[8,2,1024]{2,1,0:T(2,128)(2,1)S(1)}, u32[]{:S(2)}, u32[]{:S(2)}) async-start(bf16[8,2,1024]{2,1,0:T(2,128)(2,1)} %divide_convert_fusion), calls=%async_computation.3 | async-start | bytes 65536 | tf_op jit(solution)/shard_map/all_to_all | solution.py:79
  333.2 5.6 %all-to-all-done.3 = bf16[8,2,1024]{2,1,0:T(2,128)(2,1)S(1)} async-done(((bf16[8,2,1024]{2,1,0:T(2,128)(2,1)}), bf16[8,2,1024]{2,1,0:T(2,128)(2,1)S(1)}, u32[]{:S(2)}, u32[]{:S(2)}) %all-to-all-start.3) | async-done | bytes 32800 | tf_op jit(solution)/shard_map/all_to_all | solution.py:79
  (214 shorter events, 63.5 us)
Async XLA Ops:
  7.2 92.2 %all-gather.2.cloned.1.call-start = ((), (), s32[]{:S(2)}) async-start(), calls=%async_computation.4 | async-start | bytes 2129920 | tf_op jit(solution)/shard_map/all_gather | solution.py:46
  192.7 130.9 %all-to-all-start.1 = ((f32[64,16,1024]{2,1,0:T(8,128)}), f32[64,16,1024]{2,1,0:T(8,128)}, u32[]{:S(2)}, u32[]{:S(2)}) async-start(f32[64,16,1024]{2,1,0:T(8,128)} %bitcast.46), calls=%async_computation.1 | async-start | bytes 8388608 | tf_op jit(solution)/shard_map/all_to_all | solution.py:62
  328.2 10.5 %all-to-all-start.3 = ((bf16[8,2,1024]{2,1,0:T(2,128)(2,1)}), bf16[8,2,1024]{2,1,0:T(2,128)(2,1)S(1)}, u32[]{:S(2)}, u32[]{:S(2)}) async-start(bf16[8,2,1024]{2,1,0:T(2,128)(2,1)} %divide_convert_fusion), calls=%async_computation.3 | async-start | bytes 65536 | tf_op jit(solution)/shard_map/all_to_all | solution.py:79
Sparse Core Ops, SparseCore 0:
  19.6 79.7 all-gather.1
where the time goes:
time: 348 us; the launch traced here: 346 us
  waiting for transfers between devices  191 us (55%)
  local copies, waits for them, and re-layouts  60.1 us (17%)
  blocking collectives  27.8 us (8%)
  other arithmetic  23.3 us (7%)
  starting transfers between devices  16.3 us (5%)
  between operations  14.1 us (4%)
  matrix products  12.4 us (4%)
    all_to_all x1, waiting for transfers between devices, shards(): lax.all_to_all(partial_out.reshape(count, block, heads * head_dim), 'ctx'...  109 us
    all_gather x1, waiting for transfers between devices, shards(): piece = lax.all_gather(queries, 'ctx', axis=0, tiled=True)  76.2 us
    all_to_all x1, blocking collectives, shards(): lax.all_to_all(partial_lse.reshape(count, block, heads), 'ctx', split_axi...  16.2 us
    dynamic_slice x16, local copies, waits for them, and re-layouts, one_block(): part = lax.dynamic_slice_in_dim(piece, index * width, width, 0)  14.7 us
    dynamic_update_slice x16, local copies, waits for them, and re-layouts, one_block(): outs = lax.dynamic_update_slice_in_dim(outs, mixed, offset, 0)  12.2 us
    dynamic_slice x16, local copies, waits for them, and re-layouts, one_block(): part_seg = lax.dynamic_slice_in_dim(segment_ids, offset, width, 0)  12.2 us
    all_to_all x1, starting transfers between devices, shards(): lax.all_to_all(partial_out.reshape(count, block, heads * head_dim), 'ctx'...  12 us
    all_to_all x1, blocking collectives, shards(): lax.all_to_all(q_new, 'tp', split_axis=1, concat_axis=0, tiled=True)  11.6 us
  transfers between devices with their start and end apart: 3, of which 3 were waited for; matrix products, arithmetic and copies ran while one was open for 4% of the time, Pallas kernels for 0%

commit v1 on v0

--- a/solution.py
+++ b/solution.py
@@ -43,7 +43,9 @@
         jnp.zeros((total_rows, heads * head_dim), jnp.float32),
         jnp.zeros((total_rows, heads), jnp.float32),
     )
-    piece = lax.all_gather(queries, "ctx", axis=0, tiled=True)
+    piece = jnp.concatenate(
+        lax.all_to_all(jnp.stack([queries] * lax.axis_size("ctx")), "ctx", 0, 0), axis=0
+    )
     rows = piece.shape[0]
     width = 64
 

time: 348 us -> 323 us (0.928)
  the two profiles are of different devices: /device:TPU:272 before, /device:TPU:288 now
where the time goes in v1:
time: 323 us; the launch traced here: 322 us
  waiting for transfers between devices  160 us (50%)
  local copies, waits for them, and re-layouts  46 us (14%)
  starting transfers between devices  42.3 us (13%)
  other arithmetic  33.4 us (10%)
  blocking collectives  26.5 us (8%)
  matrix products  12.4 us (4%)
    all_to_all x1, waiting for transfers between devices, shards(): lax.all_to_all(partial_out.reshape(count, block, heads * head_dim), 'ctx'...  107 us
    all_to_all x1, waiting for transfers between devices, shards(): lax.all_to_all(jnp.stack([queries] * lax.axis_size('ctx')), 'ctx', 0, 0)  46.5 us
    all_to_all x1, blocking collectives, shards(): lax.all_to_all(partial_lse.reshape(count, block, heads), 'ctx', split_axi...  15.7 us
    all_to_all x1, starting transfers between devices, shards(): lax.all_to_all(partial_out.reshape(count, block, heads * head_dim), 'ctx'...  15.1 us
    all_to_all x1, starting transfers between devices, shards(): lax.all_to_all(final.astype(jnp.bfloat16), 'tp', split_axis=0, concat_axi...  14.4 us
    all_to_all x1, starting transfers between devices, shards(): lax.all_to_all(jnp.stack([queries] * lax.axis_size('ctx')), 'ctx', 0, 0)  12.8 us
    dynamic_update_slice x16, local copies, waits for them, and re-layouts, one_block(): outs = lax.dynamic_update_slice_in_dim(outs, mixed, offset, 0)  12.2 us
    dynamic_slice x16, local copies, waits for them, and re-layouts, one_block(): part_seg = lax.dynamic_slice_in_dim(segment_ids, offset, width, 0)  12.2 us
  transfers between devices with their start and end apart: 3, of which 3 were waited for; matrix products, arithmetic and copies ran while one was open for 4% of the time, Pallas kernels for 0%

profile of v1, /device:TPU:288, one launch (start us, length us, event | category | flops | bytes accessed | tf_op | source)
XLA Modules:
  0.0 321.7 jit_solution(11147633082476388669)
XLA Ops:
  0.7 10.8 %all_to_all.47 = bf16[2,8,1024]{2,0,1:T(2,128)(2,1)S(1)} all-to-all(bf16[2,8,1024]{2,0,1:T(2,128)(2,1)} %bitcast.55), channel_id=1, replica_groups=mesh['ctx'=64,'tp'=8] {'tp'}, dimensions={1} | all-to-all | bytes 65536 | tf_op jit(solution)/shard_map/all_to_all | solution.py:35
  11.5 1.6 stack.5
  13.1 12.8 %all-to-all-start.1 = ((bf16[64,16,1024]{2,1,0:T(8,128)(2,1)}), bf16[64,16,1024]{2,1,0:T(8,128)(2,1)S(1)}, u32[]{:S(2)}, u32[]{:S(2)}) async-start(bf16[64,16,1024]{2,1,0:T(8,128)(2,1)} %stack.5), calls=%async_computation.1 | async-start | bytes 4194304 | tf_op jit(solution)/shard_map/all_to_all | solution.py:47
  27.3 46.5 %all-to-all-done.1 = bf16[64,16,1024]{2,1,0:T(8,128)(2,1)S(1)} async-done(((bf16[64,16,1024]{2,1,0:T(8,128)(2,1)}), bf16[64,16,1024]{2,1,0:T(8,128)(2,1)S(1)}, u32[]{:S(2)}, u32[]{:S(2)}) %all-to-all-start.1) | async-done | bytes 2097184 | tf_op jit(solution)/shard_map/all_to_all | solution.py:47
  73.8 2.5 broadcast_in_dim.61
  76.3 0.8 broadcast_in_dim.62
  77.1 69.2 %while.15 = (s32[]{:T(128)}, f32[1024,1024]{1,0:T(8,128)}, f32[1024,8]{1,0:T(8,128)}, s32[]{:T(128)}, s32[16]{0:T(128)S(1)}, /*index=5*/s32[1024]{0:T(1024)}, bf...) while((s32[]{:T(128)}, f32[1024,1024]{1,0:T(8,128)}, ...), condition=%wide.region_3.4_spmd, body=%wide.region_0.3_spmd.sunk | while | flops 136152032 | bytes 4979591 | solution.py:62
  78.0 0.8 dynamic_slice.26
  82.3 0.8 dynamic_slice.26
  86.6 0.8 dynamic_slice.26
  88.6 0.8 bitcast_dynamic-update-slice_fusion.2
  92.9 0.8 bitcast_dynamic-update-slice_fusion.2
  95.2 0.8 dynamic_slice.26
  97.3 0.8 bitcast_dynamic-update-slice_fusion.2
  99.6 0.8 dynamic_slice.26
  101.6 0.8 bitcast_dynamic-update-slice_fusion.2
  103.9 0.8 dynamic_slice.26
  105.9 0.8 bitcast_dynamic-update-slice_fusion.2
  110.3 0.8 bitcast_dynamic-update-slice_fusion.2
  114.6 0.8 bitcast_dynamic-update-slice_fusion.2
  123.3 0.8 bitcast_dynamic-update-slice_fusion.2
  127.6 0.8 bitcast_dynamic-update-slice_fusion.2
  144.9 0.8 bitcast_dynamic-update-slice_fusion.2
  146.3 1.2 copy.28
  147.7 15.7 %all_to_all.48 = f32[64,1,128]{2,1,0:T(1,128)S(1)} all-to-all(f32[64,1,128]{2,1,0:T(1,128)S(1)} %reshape.115), channel_id=1, replica_groups=mesh['ctx'=64,'tp'=8] {'ctx'}, dimensions={0} | all-to-all | bytes 65536 | tf_op jit(solution)/shard_map/all_to_all | solution.py:71
  163.4 15.1 %all-to-all-start.2 = ((f32[64,16,1024]{2,1,0:T(8,128)}), f32[64,16,1024]{2,1,0:T(8,128)}, u32[]{:S(2)}, u32[]{:S(2)}) async-start(f32[64,16,1024]{2,1,0:T(8,128)} %bitcast.47), calls=%async_computation.2 | async-start | bytes 8388608 | tf_op jit(solution)/shard_map/all_to_all | solution.py:64
  180.7 2.6 mul.30
  183.3 4.9 %mul.31 = f32[64,16,1024]{2,1,0:T(8,128)} reshape(f32[64,16,8,128]{3,2,1,0:T(8,128)} %mul.30) | data formatting | bytes 8388608 | tf_op jit(solution)/shard_map/mul | solution.py:78
  188.3 107.4 %all-to-all-done.2 = f32[64,16,1024]{2,1,0:T(8,128)} async-done(((f32[64,16,1024]{2,1,0:T(8,128)}), f32[64,16,1024]{2,1,0:T(8,128)}, u32[]{:S(2)}, u32[]{:S(2)}) %all-to-all-start.2) | async-done | bytes 4194336 | tf_op jit(solution)/shard_map/all_to_all | solution.py:64
  295.7 4.0 %multiply_reduce_fusion = f32[16,1024]{1,0:T(8,128)S(1)} fusion(f32[64,16,1024]{2,1,0:T(8,128)} %all-to-all-done.2, f32[64,16,1024]{2,1,0:T(8,128)} %mul.31), kind=kLoop, calls=%fused_computation.16 | loop fusion | flops 2080768 | bytes 8454144 | tf_op jit(solution)/shard_map/reduce_sum | solution.py:78
  300.4 14.4 %all-to-all-start.4 = ((bf16[8,2,1024]{2,1,0:T(2,128)(2,1)}), bf16[8,2,1024]{2,1,0:T(2,128)(2,1)S(1)}, u32[]{:S(2)}, u32[]{:S(2)}) async-start(bf16[8,2,1024]{2,1,0:T(2,128)(2,1)} %divide_convert_fusion), calls=%async_computation.4 | async-start | bytes 65536 | tf_op jit(solution)/shard_map/all_to_all | solution.py:81
  315.5 5.6 %all-to-all-done.4 = bf16[8,2,1024]{2,1,0:T(2,128)(2,1)S(1)} async-done(((bf16[8,2,1024]{2,1,0:T(2,128)(2,1)}), bf16[8,2,1024]{2,1,0:T(2,128)(2,1)S(1)}, u32[]{:S(2)}, u32[]{:S(2)}) %all-to-all-start.4) | async-done | bytes 32800 | tf_op jit(solution)/shard_map/all_to_all | solution.py:81
  (220 shorter events, 62.0 us)
Async XLA Ops:
  0.6 25.2 %copy-start.2 = (s32[64]{0:T(128)S(1)}, s32[64]{0:T(128)}, u32[]{:S(2)}) copy-start(s32[64]{0:T(128)} %param.10) | copy-start | bytes 772
  0.6 26.6 %copy-start.1 = (bf16[2,16,128]{2,1,0:T(8,128)(2,1)S(1)}, bf16[2,16,128]{2,1,0:T(8,128)(2,1)}, u32[]{:S(2)}) copy-start(bf16[2,16,128]{2,1,0:T(8,128)(2,1)} %param.8) | copy-start | bytes 24580
  0.7 26.6 %copy-start = (bf16[2,496,128]{2,1,0:T(8,128)(2,1)S(1)}, bf16[2,496,128]{2,1,0:T(8,128)(2,1)}, u32[]{:S(2)}) copy-start(bf16[2,496,128]{2,1,0:T(8,128)(2,1)} %param.9) | copy-start | bytes 761860
  13.1 60.7 %all-to-all-start.1 = ((bf16[64,16,1024]{2,1,0:T(8,128)(2,1)}), bf16[64,16,1024]{2,1,0:T(8,128)(2,1)S(1)}, u32[]{:S(2)}, u32[]{:S(2)}) async-start(bf16[64,16,1024]{2,1,0:T(8,128)(2,1)} %stack.5), calls=%async_computation.1 | async-start | bytes 4194304 | tf_op jit(solution)/shard_map/all_to_all | solution.py:47
  163.4 132.3 %all-to-all-start.2 = ((f32[64,16,1024]{2,1,0:T(8,128)}), f32[64,16,1024]{2,1,0:T(8,128)}, u32[]{:S(2)}, u32[]{:S(2)}) async-start(f32[64,16,1024]{2,1,0:T(8,128)} %bitcast.47), calls=%async_computation.2 | async-start | bytes 8388608 | tf_op jit(solution)/shard_map/all_to_all | solution.py:64
  300.4 20.7 %all-to-all-start.4 = ((bf16[8,2,1024]{2,1,0:T(2,128)(2,1)}), bf16[8,2,1024]{2,1,0:T(2,128)(2,1)S(1)}, u32[]{:S(2)}, u32[]{:S(2)}) async-start(bf16[8,2,1024]{2,1,0:T(2,128)(2,1)} %divide_convert_fusion), calls=%async_computation.4 | async-start | bytes 65536 | tf_op jit(solution)/shard_map/all_to_all | solution.py:81
